TPU v7x, 32 devices: a whole 2x2x4 slice. The times are simulated.
32 devices in a mesh: dp: 2 (over y), slab: 4 (over z), view: 4 (over x, core).
Axes of the slice: x: 2, y: 2, z: 4, core: 2. Of those that a mesh axis runs over, the one named last changes fastest.
Arguments:
- latent_feats: bfloat16 [2, 4, 16, 32, 256], P('dp', 'view', 'slab'), may hold values from -6 to 6
- conv_weight: bfloat16 [2304, 256], P(('dp', 'slab')), may hold values from -0.125 to 0.125
- kv_weight: bfloat16 [256, 1536], P(('dp', 'slab')), may hold values from -0.375 to 0.375
- stream: bfloat16 [2, 4, 16, 32, 768], P('dp', 'view', 'slab'), may hold values from -6 to 6
- queries: bfloat16 [2, 4, 16, 32, 768], P('dp', 'view', 'slab'), may hold values from -102 to 102
- norm_gain: float32 [768], replicated, may hold values from 0.1 to 1.9
- up_weight: bfloat16 [768, 3072], P(('dp', 'slab'), 'view'), may hold values from -0.21875 to 0.21875
- down_weight: bfloat16 [768, 3072], P(('dp', 'slab'), 'view'), may hold values from -0.109375 to 0.109375
- band_start: int32 [2, 4, 16, 4], P('dp', 'view', 'slab'), may hold values from 0 to 15, as said below
- band_end: int32 [2, 4, 16, 4], P('dp', 'view', 'slab'), may hold values from 1 to 16
- visibility: int32 [2, 4, 4], P('dp'), may hold values 0 or 1
Outputs:
- output: bfloat16 [2, 4, 16, 32, 768], P('dp', 'view', 'slab')
Inputs may be any that keep to these rules, and one draw needn't show every extreme that they name: band_end - band_start lies in 1 to 4 and equals 4 for some rows in every draw; for a row r both bounds lie within rows (r // 4) * 4 - 1 to (r // 4 + 1) * 4 + 1, clipped to the grid.
All inputs are finite; a program needn't handle non-finite values. No bound on the sum of `visibility` on one device may be relied on, other than what follows from the above.
Results may differ from a plain program's by a relative error of at most 0.0085.
Values may be sent and summed in bfloat16 or wider, within the bound.
A program may use at most 64 MiB of HBM per device.

v0:
```python
import jax
import jax.numpy as jnp
from jax import lax
from jax.sharding import PartitionSpec as P

HEADS = 12
HEAD_DIM = 64
HALO = 1


def with_halo(cells, sides, width):
    for axis, dim in sides:
        count = lax.axis_size(axis)
        ends = count - 1
        head = lax.slice_in_dim(cells, 0, width, axis=dim)
        tail = lax.slice_in_dim(cells, cells.shape[dim] - width, cells.shape[dim], axis=dim)
        cells = jnp.concatenate(
            [
                lax.ppermute(tail, axis, [(i, (i + 1) % count) for i in range(ends)]),
                cells,
                lax.ppermute(head, axis, [((i + 1) % count, i) for i in range(ends)]),
            ],
            axis=dim,
        )
    return cells


def conv_block(view_feats, conv_full):
    row_count, col_count, channels = view_feats.shape
    padded = with_halo(view_feats, (("slab", 0),), 1)
    padded = jnp.pad(padded, ((0, 0), (1, 1), (0, 0)))
    running = jnp.zeros((row_count * col_count, channels), jnp.float32)
    for tap_index in range(9):
        row_off = tap_index // 3
        col_off = tap_index % 3
        window = padded[row_off : row_off + row_count, col_off : col_off + col_count].reshape(
            -1, channels
        )
        taps = conv_full[tap_index * channels : (tap_index + 1) * channels]
        running = running + jnp.dot(window, taps, preferred_element_type=jnp.float32)
    summed = view_feats.reshape(-1, channels).astype(jnp.float32) + jax.nn.silu(running)
    return summed.astype(jnp.bfloat16).reshape(row_count, col_count, channels)


def shards(
    latent_feats,
    conv_weight,
    kv_weight,
    stream,
    queries,
    norm_gain,
    up_weight,
    down_weight,
    band_start,
    band_end,
    visibility,
):
    row_count = latent_feats.shape[2]
    col_count = latent_feats.shape[3]
    channels = latent_feats.shape[4]
    model_width = stream.shape[4]
    view_count = lax.axis_size("view")
    view_id = lax.axis_index("view")
    first_row = lax.axis_index("slab") * row_count
    q_count = row_count * col_count
    conv_full, kv_full = (
        lax.all_gather(conv_weight, ("dp", "slab"), axis=0, tiled=True),
        lax.all_gather(kv_weight, ("dp", "slab"), axis=0, tiled=True),
    )
    encoded = conv_block(latent_feats[0, 0], conv_full)
    rimmed = with_halo(encoded, (("slab", 0),), HALO)
    nearby = lax.all_gather(rimmed[None], "view", axis=0, tiled=True)
    near_rows = nearby.shape[1]
    projected = jnp.dot(nearby.reshape(-1, channels), kv_full, preferred_element_type=jnp.float32)
    projected = projected.astype(jnp.bfloat16)
    k_count = projected.shape[0]
    group_count = HEADS // 4
    key_groups = (
        projected[:, :model_width].reshape(k_count, group_count, 4, HEAD_DIM).transpose(1, 0, 2, 3)
    )
    value_groups = (
        projected[:, model_width:].reshape(k_count, group_count, 4, HEAD_DIM).transpose(1, 0, 2, 3)
    )
    query_groups = queries[0, 0].reshape(q_count, group_count, 4, HEAD_DIM).transpose(1, 0, 2, 3)
    key_rows = first_row - HALO + jnp.arange(near_rows, dtype=jnp.int32)
    block_starts = band_start[0, 0]
    block_ends = band_end[0, 0]
    view_ids = jnp.arange(view_count, dtype=jnp.int32)
    vis_row = jnp.sum(jnp.where((view_ids == view_id)[:, None], visibility[0], 0), axis=0)
    seen = (view_ids == view_id) | (vis_row == 1)
    inside = (block_starts[:, :, None] <= key_rows) & (key_rows < block_ends[:, :, None])
    allowed = inside & seen[None, :, None]
    allowed = jnp.broadcast_to(
        allowed[:, None, :, :, None], (row_count, col_count, view_count, near_rows, col_count)
    )
    allowed = allowed.reshape(q_count, k_count)

    def one_group(operands):
        query_group, key_group, value_group = operands
        scores = jnp.einsum(
            "qhd,khd->hqk", query_group, key_group, preferred_element_type=jnp.float32
        )
        scores = jnp.where(allowed[None], scores * HEAD_DIM ** (-0.5), -1e30)
        highest = jnp.max(scores, axis=-1, keepdims=True)
        weights = jnp.exp(scores - highest)
        probs = (weights / jnp.sum(weights, axis=-1, keepdims=True)).astype(jnp.bfloat16)
        return jnp.einsum("hqk,khd->qhd", probs, value_group, preferred_element_type=jnp.float32)

    outputs = lax.map(one_group, (query_groups, key_groups, value_groups))
    attended = outputs.transpose(1, 0, 2, 3).reshape(q_count, model_width)
    residual = stream[0, 0].reshape(q_count, model_width).astype(jnp.float32) + attended
    square_mean = jnp.mean(residual * residual, axis=-1, keepdims=True)
    normed = (residual * lax.rsqrt(square_mean + 1e-06) * norm_gain).astype(jnp.bfloat16)
    all_tokens = lax.all_gather(normed, "view", axis=0, tiled=True)
    hidden_sum = jnp.dot(
        all_tokens,
        lax.all_gather(up_weight, ("dp", "slab"), axis=0, tiled=True),
        preferred_element_type=jnp.float32,
    )
    hidden = jax.nn.gelu(hidden_sum, approximate=True).astype(jnp.bfloat16)
    token_terms = lax.dot_general(
        hidden,
        lax.all_gather(down_weight, ("dp", "slab"), axis=0, tiled=True),
        (((1,), (1,)), ((), ())),
        preferred_element_type=jnp.float32,
    )
    mixed = lax.psum_scatter(
        token_terms.astype(jnp.bfloat16), "view", scatter_dimension=0, tiled=True
    ).astype(jnp.float32)
    result = (residual + mixed).astype(jnp.bfloat16)
    return result.reshape(1, 1, row_count, col_count, model_width)


def solution(mesh):
    return jax.shard_map(
        shards,
        mesh=mesh,
        in_specs=(
            P("dp", "view", "slab", None, None),
            P(("dp", "slab"), None),
            P(("dp", "slab"), None),
            P("dp", "view", "slab", None, None),
            P("dp", "view", "slab", None, None),
            P(),
            P(("dp", "slab"), "view"),
            P(("dp", "slab"), "view"),
            P("dp", "view", "slab", None),
            P("dp", "view", "slab", None),
            P("dp", None, None),
        ),
        out_specs=P("dp", "view", "slab", None, None),
        check_vma=False,
    )
```

profile of v0, /device:TPU:0, one launch (start us, length us, event | category | flops | bytes accessed | tf_op | source)
XLA Modules:
  0.0 175.0 jit_solution(16529450741419887711)
XLA Ops:
  6.6 0.7 all-gather.5.cloned.1.call-update
  7.3 0.7 all-gather.7.cloned.1.call-update
  8.1 0.7 slice_bitcast_fusion.3
  8.8 4.9 %collective-permute-start = (bf16[1,32,256]{2,1,0:T(8,128)(2,1)S(1)}, bf16[1,32,256]{2,1,0:T(8,128)(2,1)S(1)}, u32[]{:S(2)}, u32[]{:S(2)}) collective-permute-start(bf16[1,32,256]{2,1,0:T(8,128)(2,1)S(1)} %get-tuple-element.89), channel_id=1, source_target_pairs={{0,4},{4,8},{8,12},{1,5},{5,9},{9,13},{2,6},{6,10},{10,14},{3,7},{... | collective-permute-start | bytes 49160 | tf_op jit(solution)/shard_map/ppermute | solution.py:19
  13.8 1.3 collective-permute-start.1
  15.1 39.7 %all_gather.20 = bf16[256,1536]{1,0:T(8,128)(2,1)S(1)} all-gather(bf16[32,1536]{1,0:T(8,128)(2,1)} %param.15), channel_id=1, replica_groups=mesh['dp'=2,'slab'=4,'view'=4] {'dp','slab'}, dimensions={0}, use_global_device_ids=true | all-gather | bytes 884736 | tf_op jit(solution)/shard_map/all_gather | solution.py:68
  55.3 1.1 all-gather.5.cloned.1.call-done
  56.3 1.2 fusion.73
  57.5 1.1 fusion.64
  58.6 1.1 convolution_add_fusion.6
  59.7 1.1 convolution_add_fusion.5
  60.7 0.2 convolution_add_fusion.4
  61.1 0.2 convolution_add_fusion.2
  61.3 0.2 convolution_add_fusion.1
  61.4 0.2 add_convert_fusion.1
  61.7 3.0 %collective-permute-start.2 = (bf16[1,32,256]{2,1,0:T(8,128)(2,1)S(1)}, bf16[1,32,256]{2,1,0:T(8,128)(2,1)S(1)}, u32[]{:S(2)}, u32[]{:S(2)}) collective-permute-start(bf16[1,32,256]{2,1,0:T(8,128)(2,1)S(1)} %get-tuple-element.85), channel_id=1, source_target_pairs={{0,4},{4,8},{8,12},{1,5},{5,9},{9,13},{2,6},{6,10},{10,14},{3,7},{... | collective-permute-start | bytes 49160 | tf_op jit(solution)/shard_map/ppermute | solution.py:19
  64.6 1.3 collective-permute-start.3
  66.0 0.2 reshape_squeeze.8
  66.3 0.2 copy.30
  66.5 0.3 reshape.102
  66.9 0.3 copy.32
  67.2 3.1 %collective-permute-done.3 = bf16[1,32,256]{2,1,0:T(8,128)(2,1)S(1)} collective-permute-done((bf16[1,32,256]{2,1,0:T(8,128)(2,1)S(1)}, bf16[1,32,256]{2,1,0:T(8,128)(2,1)S(1)}, u32[]{:S(2)}, u32[]{:S(2)}) %collective-permute-start.3) | collective-permute-done | bytes 16416 | tf_op jit(solution)/shard_map/ppermute | solution.py:21
  70.3 6.4 %all-gather = bf16[24,32,256]{2,1,0:T(8,128)(2,1)S(1)} all-gather(bf16[6,32,256]{2,1,0:T(8,128)(2,1)S(1)} %pad_maximum_fusion), channel_id=2, replica_groups=mesh['dp'=2,'slab'=4,'view'=4] {'view'}, dimensions={0}, use_global_device_ids=true | all-gather | bytes 491520 | tf_op jit(solution)/shard_map/all_gather | solution.py:72
  76.7 0.8 convolution_convert_fusion
  77.7 1.4 copy.26
  79.1 0.6 copy.27
  79.7 11.2 %while.11 = (s32[]{:T(128)}, f32[3,128,4,64]{1,3,2,0:T(8,128)S(1)}, bf16[3,768,4,64]{1,3,2,0:T(8,128)(2,1)}, bf16[3,128,4,64]{1,3,2,0:T(8,128)(2,1)S(1)}, bf16[3...) while((s32[]{:T(128)}, f32[3,128,4,64]{1,3,2,0:T(8,128)S(1)}, ...), condition=%wide.region_4.5_spmd.clone, body=%wide.region_1.4_spmd.clone.sunk | while | flops 154535936 | bytes 2137261 | solution.py:109
  79.8 0.3 broadcast_in_dim.97
  80.0 0.5 broadcast_in_dim.98
  80.5 0.2 copy.34
  80.7 0.8 fusion.119
  81.5 1.9 %fusion.120 = f32[3,128,4,64]{1,3,2,0:T(8,128)S(1)} fusion(f32[3,128,4,64]{1,3,2,0:T(8,128)S(1)} %get-tuple-element.136, s32[]{:T(128)} %get-tuple-element.135, f32[4,128]{1,0:T(4,128)S(1)} %fusion.119, bf16[3,768,4,64]{1,3,2,0:T(8,128)(2,1)} %get-tuple-element.144, pred[128,768]{1,0:T(8,128)(4,1)S(1)} %copy.34, ...), kind=kOutput, calls=%fused_computation.7.clone.1 | convolution fusion | flops 102630656 | bytes 1085440 | tf_op jit(solution)/shard_map/while/body/eval_jaxpr/hqk,khd->qhd/dot_general | solution.py:107
  83.5 0.3 broadcast_in_dim.97
  83.8 0.5 broadcast_in_dim.98
  84.3 0.2 copy.34
  84.5 0.8 fusion.119
  85.3 1.9 %fusion.120 = f32[3,128,4,64]{1,3,2,0:T(8,128)S(1)} fusion(f32[3,128,4,64]{1,3,2,0:T(8,128)S(1)} %get-tuple-element.136, s32[]{:T(128)} %get-tuple-element.135, f32[4,128]{1,0:T(4,128)S(1)} %fusion.119, bf16[3,768,4,64]{1,3,2,0:T(8,128)(2,1)} %get-tuple-element.144, pred[128,768]{1,0:T(8,128)(4,1)S(1)} %copy.34, ...), kind=kOutput, calls=%fused_computation.7.clone.1 | convolution fusion | flops 102630656 | bytes 1085440 | tf_op jit(solution)/shard_map/while/body/eval_jaxpr/hqk,khd->qhd/dot_general | solution.py:107
  87.2 0.3 broadcast_in_dim.97
  87.5 0.5 broadcast_in_dim.98
  88.0 0.2 copy.34
  88.2 0.8 fusion.119
  89.0 1.9 %fusion.120 = f32[3,128,4,64]{1,3,2,0:T(8,128)S(1)} fusion(f32[3,128,4,64]{1,3,2,0:T(8,128)S(1)} %get-tuple-element.136, s32[]{:T(128)} %get-tuple-element.135, f32[4,128]{1,0:T(4,128)S(1)} %fusion.119, bf16[3,768,4,64]{1,3,2,0:T(8,128)(2,1)} %get-tuple-element.144, pred[128,768]{1,0:T(8,128)(4,1)S(1)} %copy.34, ...), kind=kOutput, calls=%fused_computation.7.clone.1 | convolution fusion | flops 102630656 | bytes 1085440 | tf_op jit(solution)/shard_map/while/body/eval_jaxpr/hqk,khd->qhd/dot_general | solution.py:107
  91.3 0.4 copy-done.4
  91.8 8.7 %all_gather.21 = bf16[512,768]{1,0:T(8,128)(2,1)S(1)} all-gather(bf16[128,768]{1,0:T(8,128)(2,1)S(1)} %multiply_convert_fusion), channel_id=1, replica_groups=mesh['dp'=2,'slab'=4,'view'=4] {'view'}, dimensions={0}, use_global_device_ids=true | all-gather | bytes 983040 | tf_op jit(solution)/shard_map/all_gather | solution.py:114
  100.5 40.2 %all-gather.9.cloned.1.call-done = bf16[768,768]{1,0:T(8,128)(2,1)} async-done(((bf16[96,768]{1,0:T(8,128)(2,1)}), bf16[768,768]{1,0:T(8,128)(2,1)}) %all-gather.9.cloned.1.call-update) | async-done | bytes 1179664 | tf_op jit(solution)/shard_map/all_gather | solution.py:123
  140.7 4.1 %convolution_convert_fusion.1 = bf16[512,768]{1,0:T(8,128)(2,1)} fusion(bf16[768,768]{1,0:T(8,128)(2,1)} %all-gather.9.cloned.1.call-done, bf16[512,768]{1,0:T(8,128)(2,1)S(1)} %all_gather.21, bf16[768,768]{1,0:T(8,128)(2,1)} %all-gather.7.cloned.1.call-done), kind=kOutput, calls=%fused_computation.35 | convolution fusion | flops 1211891712 | bytes 3932160 | tf_op jit(solution)/shard_map/dot_general | solution.py:121
  144.8 22.1 %reduce-scatter.2.cloned.1.call-done = bf16[128,768]{1,0:T(8,128)(2,1)} async-done(((bf16[512,768]{1,0:T(8,128)(2,1)}), bf16[128,768]{1,0:T(8,128)(2,1)}) %reduce-scatter.2.cloned.1.call-update) | async-done | bytes 196624 | tf_op jit(solution)/shard_map/reduce_scatter | solution.py:127
  166.9 1.7 add_convert_fusion
  (44 shorter events, 1.4 us)
Async XLA Ops:
  6.5 48.6 %copy-start.2 = (bf16[1,1,4,32,256]{4,3,2,1,0:T(8,128)(2,1)S(1)}, bf16[1,1,4,32,256]{4,3,2,1,0:T(8,128)(2,1)}, u32[]{:S(2)}) copy-start(bf16[1,1,4,32,256]{4,3,2,1,0:T(8,128)(2,1)} %param.13) | copy-start | bytes 196612
  6.5 48.3 %copy-start.5 = (s32[1,4,4]{2,1,0:T(4,128)S(1)}, s32[1,4,4]{2,1,0:T(4,128)}, u32[]{:S(2)}) copy-start(s32[1,4,4]{2,1,0:T(4,128)} %param.23) | copy-start | bytes 196
  6.5 48.4 %copy-start.6 = (s32[1,1,4,4]{3,2,1,0:T(4,128)S(1)}, s32[1,1,4,4]{3,2,1,0:T(4,128)}, u32[]{:S(2)}) copy-start(s32[1,1,4,4]{3,2,1,0:T(4,128)} %param.21) | copy-start | bytes 196
  6.5 48.5 %copy-start.7 = (s32[1,1,4,4]{3,2,1,0:T(4,128)S(1)}, s32[1,1,4,4]{3,2,1,0:T(4,128)}, u32[]{:S(2)}) copy-start(s32[1,1,4,4]{3,2,1,0:T(4,128)} %param.22) | copy-start | bytes 196
  6.5 49.8 %all-gather.5.cloned.1.call-start = ((), (), s32[]{:S(2)}) async-start(), calls=%async_computation.1 | async-start | bytes 1327104 | tf_op jit(solution)/shard_map/all_gather | solution.py:67
  7.3 93.2 %all-gather.7.cloned.1.call-start = ((), (), s32[]{:S(2)}) async-start(), calls=%async_computation.2 | async-start | bytes 1327104 | tf_op jit(solution)/shard_map/all_gather | solution.py:117
  8.0 132.7 %all-gather.9.cloned.1.call-start = ((), (), s32[]{:S(2)}) async-start(), calls=%async_computation.3 | async-start | bytes 1327104 | tf_op jit(solution)/shard_map/all_gather | solution.py:123
  8.8 46.3 %collective-permute-start = (bf16[1,32,256]{2,1,0:T(8,128)(2,1)S(1)}, bf16[1,32,256]{2,1,0:T(8,128)(2,1)S(1)}, u32[]{:S(2)}, u32[]{:S(2)}) collective-permute-start(bf16[1,32,256]{2,1,0:T(8,128)(2,1)S(1)} %get-tuple-element.89), channel_id=1, source_target_pairs={{0,4},{4,8},{8,12},{1,5},{5,9},{9,13},{2,6},{6,10},{10,14},{3,7},{... | collective-permute-start | bytes 49160 | tf_op jit(solution)/shard_map/ppermute | solution.py:19
  13.8 41.4 %collective-permute-start.1 = (bf16[1,32,256]{2,1,0:T(8,128)(2,1)S(1)}, bf16[1,32,256]{2,1,0:T(8,128)(2,1)S(1)}, u32[]{:S(2)}, u32[]{:S(2)}) collective-permute-start(bf16[1,32,256]{2,1,0:T(8,128)(2,1)S(1)} %get-tuple-element.90), channel_id=1, source_target_pairs={{4,0},{8,4},{12,8},{5,1},{9,5},{13,9},{6,2},{10,6},{14,10},{7,3},{... | collective-permute-start | bytes 49160 | tf_op jit(solution)/shard_map/ppermute | solution.py:21
  15.1 151.8 %reduce-scatter.2.cloned.1.call-start = ((), (), s32[]{:S(2)}) async-start(), calls=%async_computation.4 | async-start | bytes 983040 | tf_op jit(solution)/shard_map/reduce_scatter | solution.py:127
  56.3 4.4 %copy-start.1 = (bf16[2304,256]{1,0:T(8,128)(2,1)S(1)}, bf16[2304,256]{1,0:T(8,128)(2,1)}, u32[]{:S(2)}) copy-start(bf16[2304,256]{1,0:T(8,128)(2,1)} %all-gather.5.cloned.1.call-done) | copy-start | bytes 3538948
  60.9 5.1 %copy-start.3 = (bf16[1,1,4,32,768]{4,3,2,1,0:T(8,128)(2,1)S(1)}, bf16[1,1,4,32,768]{4,3,2,1,0:T(8,128)(2,1)}, u32[]{:S(2)}) copy-start(bf16[1,1,4,32,768]{4,3,2,1,0:T(8,128)(2,1)} %param.17) | copy-start | bytes 589828
  61.4 5.1 %copy-start = (bf16[1,1,4,32,768]{4,3,2,1,0:T(8,128)(2,1)S(1)}, bf16[1,1,4,32,768]{4,3,2,1,0:T(8,128)(2,1)}, u32[]{:S(2)}) copy-start(bf16[1,1,4,32,768]{4,3,2,1,0:T(8,128)(2,1)} %param.16) | copy-start | bytes 589828
  61.7 5.5 %collective-permute-start.2 = (bf16[1,32,256]{2,1,0:T(8,128)(2,1)S(1)}, bf16[1,32,256]{2,1,0:T(8,128)(2,1)S(1)}, u32[]{:S(2)}, u32[]{:S(2)}) collective-permute-start(bf16[1,32,256]{2,1,0:T(8,128)(2,1)S(1)} %get-tuple-element.85), channel_id=1, source_target_pairs={{0,4},{4,8},{8,12},{1,5},{5,9},{9,13},{2,6},{6,10},{10,14},{3,7},{... | collective-permute-start | bytes 49160 | tf_op jit(solution)/shard_map/ppermute | solution.py:19
  64.6 5.6 %collective-permute-start.3 = (bf16[1,32,256]{2,1,0:T(8,128)(2,1)S(1)}, bf16[1,32,256]{2,1,0:T(8,128)(2,1)S(1)}, u32[]{:S(2)}, u32[]{:S(2)}) collective-permute-start(bf16[1,32,256]{2,1,0:T(8,128)(2,1)S(1)} %get-tuple-element.86), channel_id=1, source_target_pairs={{4,0},{8,4},{12,8},{5,1},{9,5},{13,9},{6,2},{10,6},{14,10},{7,3},{... | collective-permute-start | bytes 49160 | tf_op jit(solution)/shard_map/ppermute | solution.py:21
  91.0 0.7 copy-start.4
Sparse Core Ops, SparseCore 0:
  9.4 46.8 all-gather.4
  58.4 40.2 all-gather.6
  100.8 39.7 all-gather.8
  144.9 21.9 reduce-scatter.1
where the time goes:
time: 176 us; the launch traced here: 175 us
  waiting for transfers between devices  67.8 us (39%)
  blocking collectives  54.8 us (31%)
  matrix products  18.3 us (10%)
  between operations  13.4 us (8%)
  starting transfers between devices  10.7 us (6%)
  local copies, waits for them, and re-layouts  7.77 us (4%)
  other arithmetic  2.16 us (1%)
    all_gather x1, waiting for transfers between devices, shards(): lax.all_gather(down_weight, ('dp', 'slab'), axis=0, tiled=True)  40.2 us
    all_gather x1, blocking collectives, shards(): lax.all_gather(kv_weight, ('dp', 'slab'), axis=0, tiled=True)  39.7 us
    reduce_scatter x1, waiting for transfers between devices, shards(): lax.psum_scatter(token_terms.astype(jnp.bfloat16), 'view', scatter_dimens...  22.1 us
    all_gather x1, blocking collectives, shards(): all_tokens = lax.all_gather(normed, 'view', axis=0, tiled=True)  8.71 us
    ppermute x2, starting transfers between devices, with_halo(): lax.ppermute(tail, axis, [(i, (i + 1) % count) for i in range(ends)])  7.93 us
    all_gather x1, blocking collectives, shards(): nearby = lax.all_gather(rimmed[None], 'view', axis=0, tiled=True)  6.42 us
    dot_general x3, matrix products, one_group(): jnp.einsum('hqk,khd->qhd', probs, value_group, preferred_element_type=jnp...  5.81 us
    dot_general x9, matrix products, conv_block(): jnp.dot(window, taps, preferred_element_type=jnp.float32)  5.23 us
  transfers between devices with their start and end apart: 8, of which 4 were waited for; matrix products, arithmetic and copies ran while one was open for 13% of the time, Pallas kernels for 0%

commit v1 on v0

v1 whole, which is shorter than its diff:
```python
import jax
import jax.numpy as jnp
from jax import lax
from jax.experimental import pallas as pl
from jax.experimental.pallas import tpu as pltpu
from jax.sharding import PartitionSpec as P

HEAD_DIM = 64
HALO = 1
MESH = pl.DeviceIdType.MESH
CONV, KV, UP, DOWN = range(4)


def block_kernel(
    n_dp, n_slab, n_view, gather, row_count, col_count,
    feats, conv_in, kv_in, stream, queries, gain, up_in, down_in,
    starts, ends, visible,
    out,
    conv_buf, kv_buf, up_buf, down_buf, feat_buf, enc_buf, proj_buf, bias_buf,
    stream_buf, query_buf, gain_buf, res_buf, tokens, terms, sums,
    loc_sem, z_send, z_recv, y_send, y_recv, c_send, c_recv, f_send, f_recv,
    t_send, t_recv, s_send, s_recv,
):
    d = lax.axis_index("dp")
    s = lax.axis_index("slab")
    v = lax.axis_index("view")
    tokens_dev = row_count * col_count
    channels = feats.shape[1]
    width = stream.shape[1]
    edge = (HALO + 1) * col_count
    near = row_count + 2 * HALO
    half_id = lax.rem(v, 2)
    partner = v + 1 - 2 * half_id

    def view_at(i):
        chip = lax.rem(v // 2 + i // 2, n_view // 2)
        return chip * 2 + lax.rem(half_id + i % 2, 2)

    barrier = pltpu.get_barrier_semaphore()

    def hello(**where):
        pl.semaphore_signal(barrier, inc=1, device_id=where, device_id_type=MESH)

    greeted = n_view - 1
    for i in range(1, n_view):
        hello(view=view_at(i))
    side_views = range(n_view)
    if gather:
        side_views = range(1, n_view)
        greeted += n_slab - 1 + n_dp - 1
        for o in range(1, n_slab):
            hello(slab=lax.rem(s + o, n_slab))
        for i in range(1, n_dp):
            hello(dp=lax.rem(d + i, n_dp))

    @pl.when(s > 0)
    def _():
        for i in side_views:
            hello(slab=s - 1, view=view_at(i))

    @pl.when(s < n_slab - 1)
    def _():
        for i in side_views:
            hello(slab=s + 1, view=view_at(i))

    sides = jnp.where(s > 0, 1, 0) + jnp.where(s < n_slab - 1, 1, 0)
    pl.semaphore_wait(barrier, greeted + len(side_views) * sides)

    bufs = (conv_buf, kv_buf, up_buf, down_buf)
    srcs = (conv_in, kv_in, up_in, down_in)
    sends = []

    def region(w, i, o, other=False):
        rows = srcs[w].shape[0]
        k = lax.rem(d - i + n_dp, n_dp) * n_slab + lax.rem(s - o + n_slab, n_slab)
        at = pl.ds(pl.multiple_of(k * rows, 16), rows)
        if w in (UP, DOWN):
            return bufs[w].at[at]
        half = bufs[w].shape[1] // 2
        side = 1 - half_id if other else half_id
        return bufs[w].at[at, pl.ds(pl.multiple_of(side * half, 128), half)]

    def own_part(w):
        if w in (UP, DOWN):
            return srcs[w]
        half = bufs[w].shape[1] // 2
        return srcs[w].at[:, pl.ds(pl.multiple_of(half_id * half, 128), half)]

    def push(src, dst, send_sem, recv_sem, **where):
        copy = pltpu.make_async_remote_copy(
            src_ref=src, dst_ref=dst, send_sem=send_sem, recv_sem=recv_sem,
            device_id=where, device_id_type=MESH,
        )
        copy.start()
        sends.append(copy)

    def landed(dst, send_sem, recv_sem, **where):
        pltpu.make_async_remote_copy(
            src_ref=dst, dst_ref=dst, send_sem=send_sem, recv_sem=recv_sem,
            device_id=where, device_id_type=MESH,
        ).wait_recv()

    def send_z(w):
        for o in range(1, n_slab):
            push(own_part(w), region(w, 0, 0), z_send.at[w, o], z_recv.at[w, o],
                 slab=lax.rem(s + o, n_slab))

    def send_y(w):
        for i in range(1, n_dp):
            push(own_part(w), region(w, 0, 0), y_send.at[w, i, 0], y_recv.at[w, i, 0],
                 dp=lax.rem(d + i, n_dp))

    def to_core(w, i, o):
        if w in (CONV, KV):
            push(region(w, i, o), region(w, i, o), c_send.at[w, i, o], c_recv.at[w, i, o],
                 view=partner)

    def relay_z(w, o):
        landed(region(w, 0, o), z_send.at[w, o], z_recv.at[w, o],
               slab=lax.rem(s - o + n_slab, n_slab))
        for i in range(1, n_dp):
            push(region(w, 0, o), region(w, 0, o), y_send.at[w, i, o], y_recv.at[w, i, o],
                 dp=lax.rem(d + i, n_dp))
        to_core(w, 0, o)

    def take_y(w, o):
        for i in range(1, n_dp):
            landed(region(w, i, o), y_send.at[w, i, o], y_recv.at[w, i, o],
                   dp=lax.rem(d - i + n_dp, n_dp))
            to_core(w, i, o)

    def take_core(w):
        for i in range(n_dp):
            for o in range(n_slab):
                if i or o:
                    landed(region(w, i, o, True), c_send.at[w, i, o], c_recv.at[w, i, o],
                           view=partner)

    def local(src, dst, index):
        copy = pltpu.make_async_copy(src, dst, loc_sem.at[index])
        copy.start()
        return copy

    if gather:
        send_z(CONV)
        send_y(CONV)

    low = pl.ds(0, edge)
    mid = pl.ds(edge, tokens_dev)
    high = pl.ds(edge + tokens_dev, edge)

    def feat_copy(i, part):
        u = view_at(i)
        if part == 0:
            return pltpu.make_async_remote_copy(
                feats, feat_buf.at[v, mid], f_send.at[i, 0], f_recv.at[i, 0],
                device_id={"view": u}, device_id_type=MESH)
        if part == 1:
            return pltpu.make_async_remote_copy(
                feats.at[pl.ds(tokens_dev - edge, edge)], feat_buf.at[v, low],
                f_send.at[i, 1], f_recv.at[i, 1],
                device_id={"slab": s + 1, "view": u}, device_id_type=MESH)
        return pltpu.make_async_remote_copy(
            feats.at[pl.ds(0, edge)], feat_buf.at[v, high],
            f_send.at[i, 2], f_recv.at[i, 2],
            device_id={"slab": s - 1, "view": u}, device_id_type=MESH)

    own_feat = local(feats, feat_buf.at[v, mid], 0)

    def source_view(i):
        chip = lax.rem(v // 2 - i // 2 + n_view // 2, n_view // 2)
        return chip * 2 + lax.rem(half_id + i % 2, 2)

    def feat_landed(i, part):
        where = (mid, low, high)[part]
        ref = feat_buf.at[source_view(i), where]
        landed(ref, f_send.at[i, part], f_recv.at[i, part], view=source_view(1))

    for i in range(1, n_view):
        feat_copy(i, 0).start()

    @pl.when(s < n_slab - 1)
    def _():
        for i in range(n_view):
            feat_copy(i, 1).start()

    @pl.when(s > 0)
    def _():
        for i in range(n_view):
            feat_copy(i, 2).start()

    if gather:
        send_z(KV)
        send_y(KV)
    loads = [
        local(stream, stream_buf, 1),
        local(queries, query_buf, 2),
        local(gain, gain_buf, 3),
    ]
    if gather:
        weight_loads = []
        for w in range(4):
            rows = srcs[w].shape[0]
            at = pl.ds(pl.multiple_of((d * n_slab + s) * rows, 16), rows)
            weight_loads.append(local(srcs[w], bufs[w].at[at], 4 + w))
    else:
        weight_loads = [local(srcs[w], bufs[w], 4 + w) for w in range(4)]

    @pl.when(s == 0)
    def _():
        feat_buf[:, 0:edge, :] = jnp.zeros((n_view, edge, channels), jnp.bfloat16)

    @pl.when(s == n_slab - 1)
    def _():
        feat_buf[:, edge + tokens_dev:, :] = jnp.zeros((n_view, edge, channels), jnp.bfloat16)

    k_count = n_view * near * col_count
    lane = lax.broadcasted_iota(jnp.int32, (1, k_count), 1)
    key_view = jnp.zeros((1, k_count), jnp.int32)
    key_row = jnp.zeros((1, k_count), jnp.int32)
    for b in range(1, n_view * near):
        key_row = key_row + jnp.where(lane >= b * col_count, 1, 0)
    for b in range(1, n_view):
        key_view = key_view + jnp.where(lane >= b * near * col_count, 1, 0)
    key_row = key_row - near * key_view + (s * row_count - HALO)
    seen = jnp.zeros((1, k_count), jnp.int32)
    for u in range(n_view):
        flag = jnp.where(v == u, 1, visible[0, v, u])
        seen = jnp.where(key_view == u, flag, seen)
    for r in range(row_count):
        first = jnp.zeros((1, k_count), jnp.int32)
        last = jnp.zeros((1, k_count), jnp.int32)
        for u in range(n_view):
            first = jnp.where(key_view == u, starts[0, 0, r, u], first)
            last = jnp.where(key_view == u, ends[0, 0, r, u], last)
        fits = jnp.where(key_row >= first, 1, 0) * jnp.where(key_row < last, 1, 0)
        fits = fits * jnp.where(seen == 1, 1, 0)
        addend = jnp.where(fits == 1, 0.0, -1e30)
        bias_buf[r * col_count:(r + 1) * col_count, :] = jnp.broadcast_to(
            addend, (col_count, k_count))

    if gather:
        take_y(CONV, 0)
        for o in range(1, n_slab):
            relay_z(CONV, o)
        send_z(UP)
        send_y(UP)
        take_y(KV, 0)
        for o in range(1, n_slab):
            relay_z(KV, o)
        for o in range(1, n_slab):
            take_y(CONV, o)
        send_z(DOWN)
        send_y(DOWN)
        for o in range(1, n_slab):
            take_y(KV, o)
    own_feat.wait()
    for i in range(1, n_view):
        feat_landed(i, 0)

    @pl.when(s > 0)
    def _():
        for i in range(n_view):
            feat_landed(i, 1)

    @pl.when(s < n_slab - 1)
    def _():
        for i in range(n_view):
            feat_landed(i, 2)

    weight_loads[CONV].wait()
    if gather:
        take_core(CONV)

    span = near * col_count
    count = (row_count + 2 * (HALO + 1)) * col_count
    column = lax.broadcasted_iota(jnp.int32, (count, channels), 0) & (col_count - 1)
    for u in range(n_view):
        x = feat_buf[u]
        wide = x.astype(jnp.float32)
        before = jnp.where(column == 0, 0.0, pltpu.roll(wide, 1, 0)).astype(jnp.bfloat16)
        after = jnp.where(column == col_count - 1, 0.0, pltpu.roll(wide, count - 1, 0)).astype(
            jnp.bfloat16)
        taps = [
            part[row * col_count:row * col_count + span]
            for row in range(3) for part in (before, x, after)
        ]
        running = jnp.dot(jnp.concatenate(taps, axis=1), conv_buf[...],
                          preferred_element_type=jnp.float32)
        gated = running / (1.0 + jnp.exp(-running))
        enc_buf[u * span:(u + 1) * span, :] = (
            wide[HALO * col_count:HALO * col_count + span] + gated).astype(jnp.bfloat16)

    weight_loads[KV].wait()
    if gather:
        take_core(KV)
    for u in range(n_view):
        proj_buf[u * span:(u + 1) * span, :] = jnp.dot(
            enc_buf[u * span:(u + 1) * span, :], kv_buf[...],
            preferred_element_type=jnp.float32).astype(jnp.bfloat16)

    for copy in loads:
        copy.wait()

    per = 256 // HEAD_DIM
    head_of = lax.broadcasted_iota(jnp.int32, (tokens_dev, per * HEAD_DIM), 1) // HEAD_DIM
    total = jnp.zeros((tokens_dev, 1), jnp.float32)
    for g in range(width // (per * HEAD_DIM)):
        if gather and g + 1 < n_slab:
            relay_z(UP, g + 1)
        at = slice(g * per * HEAD_DIM, (g + 1) * per * HEAD_DIM)
        query = query_buf[:, at] * jnp.bfloat16(HEAD_DIM ** -0.5)
        stack = jnp.concatenate(
            [jnp.where(head_of == h, query, jnp.bfloat16(0)) for h in range(per)], axis=0)
        scores = lax.dot_general(stack, proj_buf[:, at], (((1,), (1,)), ((), ())),
                                 preferred_element_type=jnp.float32)
        value = proj_buf[:, width + g * per * HEAD_DIM:width + (g + 1) * per * HEAD_DIM]
        attended = jnp.zeros((tokens_dev, per * HEAD_DIM), jnp.float32)
        for h in range(per):
            part = scores[h * tokens_dev:(h + 1) * tokens_dev] + bias_buf[...]
            weights = jnp.exp(part - jnp.max(part, axis=1, keepdims=True))
            inverse = 1.0 / jnp.sum(weights, axis=1, keepdims=True)
            probs = (weights * inverse).astype(jnp.bfloat16)
            mixed = jnp.dot(probs, value, preferred_element_type=jnp.float32)
            attended = jnp.where(head_of == h, mixed, attended)
        residual = stream_buf[:, at].astype(jnp.float32) + attended
        res_buf[:, at] = residual
        total = total + jnp.sum(residual * residual, axis=1, keepdims=True)
    scale = lax.rsqrt(total * (1.0 / width) + 1e-06)
    tokens[v] = (res_buf[...] * scale * gain_buf[...]).astype(jnp.bfloat16)
    for i in range(1, n_view):
        push(tokens.at[v], tokens.at[v], t_send.at[i], t_recv.at[i], view=view_at(i))
    if gather:
        for o in range(width // (per * HEAD_DIM) + 1, n_slab):
            relay_z(UP, o)
        for o in range(1, n_slab):
            relay_z(DOWN, o)
        for o in range(n_slab):
            take_y(UP, o)
    weight_loads[UP].wait()

    def unit(u):
        return jax.nn.gelu(
            jnp.dot(tokens[u], up_buf[...], preferred_element_type=jnp.float32),
            approximate=True).astype(jnp.bfloat16)

    def term(hidden):
        return lax.dot_general(hidden, down_buf[...], (((1,), (1,)), ((), ())),
                               preferred_element_type=jnp.float32).astype(jnp.bfloat16)

    own_hidden = unit(v)
    for i in range(1, n_view):
        u = source_view(i)
        landed(tokens.at[u], t_send.at[i], t_recv.at[i], view=u)
        hidden = unit(u)
        if i == 1:
            weight_loads[DOWN].wait()
            if gather:
                for o in range(n_slab):
                    take_y(DOWN, o)
        terms[i] = term(hidden)
        push(terms.at[i], sums.at[i], s_send.at[i], s_recv.at[i], view=u)
    mixed = term(own_hidden).astype(jnp.float32)
    for i in range(1, n_view):
        landed(sums.at[i], s_send.at[i], s_recv.at[i], view=view_at(i))
        mixed = mixed + sums[i].astype(jnp.float32)
    out[...] = (res_buf[...] + mixed).astype(jnp.bfloat16)

    for copy in sends:
        copy.wait_send()
    for i in range(1, n_view):
        feat_copy(i, 0).wait_send()

    @pl.when(s < n_slab - 1)
    def _():
        for i in range(n_view):
            feat_copy(i, 1).wait_send()

    @pl.when(s > 0)
    def _():
        for i in range(n_view):
            feat_copy(i, 2).wait_send()


def solution(mesh):
    n_dp, n_slab, n_view = (mesh.shape[name] for name in ("dp", "slab", "view"))

    def shards(
        latent_feats, conv_weight, kv_weight, stream, queries, norm_gain,
        up_weight, down_weight, band_start, band_end, visibility,
    ):
        row_count, col_count, channels = latent_feats.shape[2:]
        width = stream.shape[4]
        units = up_weight.shape[1]
        tokens = row_count * col_count
        group = n_dp * n_slab
        weights = [conv_weight, kv_weight, up_weight, down_weight]
        gather = all(w.shape[0] % 16 == 0 for w in weights)
        if not gather:
            weights = [lax.all_gather(w, ("dp", "slab"), axis=0, tiled=True) for w in weights]
        near = row_count + 2 * HALO
        count = row_count + 2 * (HALO + 1)
        keys = n_view * near * col_count

        def kernel(*refs):
            block_kernel(n_dp, n_slab, n_view, gather, row_count, col_count, *refs)

        anywhere = pl.BlockSpec(memory_space=pl.ANY)
        scalar = pl.BlockSpec(memory_space=pltpu.SMEM)
        half = jnp.bfloat16
        dma = pltpu.SemaphoreType.DMA
        result = pl.pallas_call(
            kernel,
            out_shape=jax.ShapeDtypeStruct((tokens, width), half),
            in_specs=[anywhere] * 8 + [scalar] * 3,
            out_specs=pl.BlockSpec(memory_space=pltpu.VMEM),
            scratch_shapes=[
                pltpu.VMEM((9 * channels, channels), half),
                pltpu.VMEM((channels, 2 * width), half),
                pltpu.VMEM((width, units), half),
                pltpu.VMEM((width, units), half),
                pltpu.VMEM((n_view, count * col_count, channels), half),
                pltpu.VMEM((keys, channels), half),
                pltpu.VMEM((keys, 2 * width), half),
                pltpu.VMEM((tokens, keys), jnp.float32),
                pltpu.VMEM((tokens, width), half),
                pltpu.VMEM((tokens, width), half),
                pltpu.VMEM((1, width), jnp.float32),
                pltpu.VMEM((tokens, width), jnp.float32),
                pltpu.VMEM((n_view, tokens, width), half),
                pltpu.VMEM((n_view, tokens, width), half),
                pltpu.VMEM((n_view, tokens, width), half),
                dma((8,)),
                dma((4, n_slab)), dma((4, n_slab)),
                dma((4, n_dp, n_slab)), dma((4, n_dp, n_slab)),
                dma((2, n_dp, n_slab)), dma((2, n_dp, n_slab)),
                dma((n_view, 3)), dma((n_view, 3)),
                dma((n_view,)), dma((n_view,)),
                dma((n_view,)), dma((n_view,)),
            ],
            compiler_params=pltpu.CompilerParams(collective_id=0, has_side_effects=True),
        )(
            latent_feats.reshape(tokens, channels), weights[0], weights[1],
            stream.reshape(tokens, width), queries.reshape(tokens, width),
            norm_gain.reshape(1, width), weights[2], weights[3],
            band_start, band_end, visibility,
        )
        return result.reshape(1, 1, row_count, col_count, width)

    return jax.shard_map(
        shards,
        mesh=mesh,
        in_specs=(
            P("dp", "view", "slab", None, None),
            P(("dp", "slab"), None),
            P(("dp", "slab"), None),
            P("dp", "view", "slab", None, None),
            P("dp", "view", "slab", None, None),
            P(),
            P(("dp", "slab"), "view"),
            P(("dp", "slab"), "view"),
            P("dp", "view", "slab", None),
            P("dp", "view", "slab", None),
            P("dp", None, None),
        ),
        out_specs=P("dp", "view", "slab", None, None),
        check_vma=False,
    )
```

time: 176 us -> 71.4 us (0.41)
  Pallas kernels: 0 us -> 67.9 us
  waiting for transfers between devices: 67.8 us -> 0 us
  blocking collectives: 54.8 us -> 0 us
  matrix products: 18.3 us -> 0 us
  between operations: 13.4 us -> 0.01 us
  starting transfers between devices: 10.7 us -> 0 us
  local copies, waits for them, and re-layouts: 7.77 us -> 2.88 us
  other arithmetic: 2.16 us -> 0 us
    pallas_call x0 -> x1, Pallas kernels: none -> 67.9 us  [shards(): pl.pallas_call(kernel, out_shape=jax.ShapeDtypeStruct((tokens, width), ha...]
    all_gather x3 -> x0, blocking collectives: 54.8 us -> none  [the longest x1 39.7 us: shards(): lax.all_gather(kv_weight, ('dp', 'slab'), axis=0, tiled=True)]
    all_gather x3 -> x0, waiting for transfers between devices: 41.3 us -> none  [the longest x1 40.2 us: shards(): lax.all_gather(down_weight, ('dp', 'slab'), axis=0, tiled=True)]
    reduce_scatter x1 -> x0, waiting for transfers between devices: 22.1 us -> none  [shards(): lax.psum_scatter(token_terms.astype(jnp.bfloat16), 'view', scatter_dimens...]
    dot_general x14 -> x0, matrix products: 15.9 us -> none  [the longest x3 5.81 us: one_group(): jnp.einsum('hqk,khd->qhd', probs, value_group, preferred_element_type=jnp...]
    ppermute x4 -> x0, starting transfers between devices: 10.5 us -> none  [the longest x2 7.93 us: with_halo(): lax.ppermute(tail, axis, [(i, (i + 1) % count) for i in range(ends)])]
    ppermute x4 -> x0, waiting for transfers between devices: 3.09 us -> none  [the longest x2 3.08 us: with_halo(): lax.ppermute(head, axis, [((i + 1) % count, i) for i in range(ends)])]
    slice x6 -> x0, local copies, waits for them, and re-layouts: 3.01 us -> none  [the longest x1 1.44 us: shards(): projected[:, model_width:].reshape(k_count, group_count, 4, HEAD_DIM)]
  transfers between devices with their start and end apart: 8 -> 0, of which waited for: 4 -> 0; matrix products, arithmetic and copies ran while one was open for 13% -> 0% of each run, Pallas kernels for 0% -> 0%
where the time goes in v1:
time: 71.4 us; the launch traced here: 70.8 us
  Pallas kernels  67.9 us (95%)
  local copies, waits for them, and re-layouts  2.88 us (4%)
    pallas_call x1, Pallas kernels, shards(): pl.pallas_call(kernel, out_shape=jax.ShapeDtypeStruct((tokens, width), ha...  67.9 us
    unnamed x3, local copies, waits for them, and re-layouts  2.3 us

profile of v1, /device:TPU:0, one launch (start us, length us, event | category | flops | bytes accessed | tf_op | source)
XLA Modules:
  0.0 70.8 jit_solution(15224379377061319370)
XLA Ops:
  0.0 0.0 copy-start
  0.0 0.7 copy-done
  0.7 0.6 reshape.18.refs_5_
  1.3 67.9 %shard_map.109 = bf16[128,768]{1,0:T(8,128)(2,1)} custom-call(bf16[128,256]{1,0:T(8,128)(2,1)} %bitcast.7, bf16[288,256]{1,0:T(8,128)(2,1)} %refs_1_.1, bf16[32,1536]{1,0:T(8,128)(2,1)} %refs_2_.1, bf16[128,768]{1,0:T(8,128)(2,1)} %bitcast.5, bf16[128,768]{1,0:T(8,128)(2,1)} %bitcast.6, f32[1,768]{1,0:T(1,128)} %reshape.18.refs_5_, bf16[96,768]{1,0:T(8,128)(2,1)} %refs_6_.1, ...), custom_call_target="tpu_custom_call" | custom-call | tf_op jit(solution)/shard_map/pallas_call | solution.py:412
  69.2 1.6 %copy.13 = bf16[1,1,4,32,768]{4,3,2,1,0:T(8,128)(2,1)} copy(bf16[1,1,4,32,768]{4,3,2,1,0:T(8,128)(2,1)} %bitcast.4) | data formatting | bytes 393216
Async XLA Ops:
  0.0 0.7 copy-start

commit v2 on v1

--- a/solution.py
+++ b/solution.py
@@ -70,15 +70,15 @@
     srcs = (conv_in, kv_in, up_in, down_in)
     sends = []
 
-    def region(w, i, o, other=False):
+    def region(w, i, side, hop, other=False):
         rows = srcs[w].shape[0]
-        k = lax.rem(d - i + n_dp, n_dp) * n_slab + lax.rem(s - o + n_slab, n_slab)
+        k = lax.rem(d - i + n_dp, n_dp) * n_slab + s + (hop if side else -hop)
         at = pl.ds(pl.multiple_of(k * rows, 16), rows)
         if w in (UP, DOWN):
             return bufs[w].at[at]
         half = bufs[w].shape[1] // 2
-        side = 1 - half_id if other else half_id
-        return bufs[w].at[at, pl.ds(pl.multiple_of(side * half, 128), half)]
+        where = 1 - half_id if other else half_id
+        return bufs[w].at[at, pl.ds(pl.multiple_of(where * half, 128), half)]
 
     def own_part(w):
         if w in (UP, DOWN):
@@ -86,55 +86,85 @@
         half = bufs[w].shape[1] // 2
         return srcs[w].at[:, pl.ds(pl.multiple_of(half_id * half, 128), half)]
 
-    def push(src, dst, send_sem, recv_sem, **where):
-        copy = pltpu.make_async_remote_copy(
-            src_ref=src, dst_ref=dst, send_sem=send_sem, recv_sem=recv_sem,
+    def only(cond, action):
+        if cond is None:
+            action()
+        else:
+            pl.when(cond)(action)
+
+    def push(cond, src, dst, send_sem, recv_sem, **where):
+        def copy():
+            return pltpu.make_async_remote_copy(
+                src_ref=src(), dst_ref=dst(), send_sem=send_sem, recv_sem=recv_sem,
+                device_id=where, device_id_type=MESH,
+            )
+
+        only(cond, lambda: copy().start())
+        sends.append((cond, copy))
+
+    def landed(cond, dst, send_sem, recv_sem, **where):
+        only(cond, lambda: pltpu.make_async_remote_copy(
+            src_ref=dst(), dst_ref=dst(), send_sem=send_sem, recv_sem=recv_sem,
             device_id=where, device_id_type=MESH,
-        )
-        copy.start()
-        sends.append(copy)
-
-    def landed(dst, send_sem, recv_sem, **where):
-        pltpu.make_async_remote_copy(
-            src_ref=dst, dst_ref=dst, send_sem=send_sem, recv_sem=recv_sem,
-            device_id=where, device_id_type=MESH,
-        ).wait_recv()
-
-    def send_z(w):
-        for o in range(1, n_slab):
-            push(own_part(w), region(w, 0, 0), z_send.at[w, o], z_recv.at[w, o],
-                 slab=lax.rem(s + o, n_slab))
-
-    def send_y(w):
+        ).wait_recv())
+
+    def there(side, hop):
+        if hop == 0:
+            return None
+        return s + hop < n_slab if side else s >= hop
+
+    def pass_z(w, side, hop, src):
+        if hop + 1 >= n_slab:
+            return
+        cond = s > 0 if side else s < n_slab - 1
+        if hop:
+            cond = jnp.logical_and(cond, there(side, hop))
+        push(cond, src, lambda: region(w, 0, side, hop),
+             z_send.at[w, side, hop + 1], z_recv.at[w, side, hop + 1],
+             slab=s - 1 if side else s + 1)
+
+    def pass_y(w, side, hop, src):
         for i in range(1, n_dp):
-            push(own_part(w), region(w, 0, 0), y_send.at[w, i, 0], y_recv.at[w, i, 0],
+            push(there(side, hop), src, lambda: region(w, 0, side, hop),
+                 y_send.at[w, i, side, hop], y_recv.at[w, i, side, hop],
                  dp=lax.rem(d + i, n_dp))
 
-    def to_core(w, i, o):
+    def to_core(w, i, side, hop):
         if w in (CONV, KV):
-            push(region(w, i, o), region(w, i, o), c_send.at[w, i, o], c_recv.at[w, i, o],
-                 view=partner)
-
-    def relay_z(w, o):
-        landed(region(w, 0, o), z_send.at[w, o], z_recv.at[w, o],
-               slab=lax.rem(s - o + n_slab, n_slab))
+            part = lambda: region(w, i, side, hop)
+            push(there(side, hop), part, part, c_send.at[w, i, side, hop],
+                 c_recv.at[w, i, side, hop], view=partner)
+
+    def send_own(w):
+        pass_z(w, 0, 0, lambda: own_part(w))
+        pass_z(w, 1, 0, lambda: own_part(w))
+        pass_y(w, 0, 0, lambda: own_part(w))
+
+    def relay_z(w, hop):
+        for side in range(2):
+            part = lambda side=side: region(w, 0, side, hop)
+            landed(there(side, hop), part, z_send.at[w, side, hop], z_recv.at[w, side, hop],
+                   slab=s + 1 if side else s - 1)
+            pass_z(w, side, hop, part)
+            pass_y(w, side, hop, part)
+            to_core(w, 0, side, hop)
+
+    def take_y(w, hop):
         for i in range(1, n_dp):
-            push(region(w, 0, o), region(w, 0, o), y_send.at[w, i, o], y_recv.at[w, i, o],
-                 dp=lax.rem(d + i, n_dp))
-        to_core(w, 0, o)
-
-    def take_y(w, o):
-        for i in range(1, n_dp):
-            landed(region(w, i, o), y_send.at[w, i, o], y_recv.at[w, i, o],
-                   dp=lax.rem(d - i + n_dp, n_dp))
-            to_core(w, i, o)
+            for side in range(2 if hop else 1):
+                landed(there(side, hop), lambda: region(w, i, side, hop),
+                       y_send.at[w, i, side, hop], y_recv.at[w, i, side, hop],
+                       dp=lax.rem(d - i + n_dp, n_dp))
+                to_core(w, i, side, hop)
 
     def take_core(w):
         for i in range(n_dp):
-            for o in range(n_slab):
-                if i or o:
-                    landed(region(w, i, o, True), c_send.at[w, i, o], c_recv.at[w, i, o],
-                           view=partner)
+            for hop in range(n_slab):
+                for side in range(2 if hop else 1):
+                    if i or hop:
+                        landed(there(side, hop), lambda: region(w, i, side, hop, True),
+                               c_send.at[w, i, side, hop], c_recv.at[w, i, side, hop],
+                               view=partner)
 
     def local(src, dst, index):
         copy = pltpu.make_async_copy(src, dst, loc_sem.at[index])
@@ -142,8 +172,7 @@
         return copy
 
     if gather:
-        send_z(CONV)
-        send_y(CONV)
+        send_own(CONV)
 
     low = pl.ds(0, edge)
     mid = pl.ds(edge, tokens_dev)
@@ -174,7 +203,7 @@
     def feat_landed(i, part):
         where = (mid, low, high)[part]
         ref = feat_buf.at[source_view(i), where]
-        landed(ref, f_send.at[i, part], f_recv.at[i, part], view=source_view(1))
+        landed(None, lambda: ref, f_send.at[i, part], f_recv.at[i, part], view=source_view(1))
 
     for i in range(1, n_view):
         feat_copy(i, 0).start()
@@ -190,8 +219,7 @@
             feat_copy(i, 2).start()
 
     if gather:
-        send_z(KV)
-        send_y(KV)
+        send_own(KV)
     loads = [
         local(stream, stream_buf, 1),
         local(queries, query_buf, 2),
@@ -240,20 +268,16 @@
             addend, (col_count, k_count))
 
     if gather:
-        take_y(CONV, 0)
-        for o in range(1, n_slab):
-            relay_z(CONV, o)
-        send_z(UP)
-        send_y(UP)
-        take_y(KV, 0)
-        for o in range(1, n_slab):
-            relay_z(KV, o)
-        for o in range(1, n_slab):
-            take_y(CONV, o)
-        send_z(DOWN)
-        send_y(DOWN)
-        for o in range(1, n_slab):
-            take_y(KV, o)
+        for hop in range(1, n_slab):
+            relay_z(CONV, hop)
+            take_y(CONV, hop - 1)
+            if hop == 1:
+                send_own(UP)
+            relay_z(KV, hop)
+            take_y(KV, hop - 1)
+        send_own(DOWN)
+        take_y(CONV, n_slab - 1)
+        take_y(KV, n_slab - 1)
     own_feat.wait()
     for i in range(1, n_view):
         feat_landed(i, 0)
@@ -293,6 +317,7 @@
 
     weight_loads[KV].wait()
     if gather:
+        relay_z(UP, 1)
         take_core(KV)
     for u in range(n_view):
         proj_buf[u * span:(u + 1) * span, :] = jnp.dot(
@@ -306,8 +331,8 @@
     head_of = lax.broadcasted_iota(jnp.int32, (tokens_dev, per * HEAD_DIM), 1) // HEAD_DIM
     total = jnp.zeros((tokens_dev, 1), jnp.float32)
     for g in range(width // (per * HEAD_DIM)):
-        if gather and g + 1 < n_slab:
-            relay_z(UP, g + 1)
+        if gather and g + 2 < n_slab:
+            relay_z(UP, g + 2)
         at = slice(g * per * HEAD_DIM, (g + 1) * per * HEAD_DIM)
         query = query_buf[:, at] * jnp.bfloat16(HEAD_DIM ** -0.5)
         stack = jnp.concatenate(
@@ -327,16 +352,17 @@
         res_buf[:, at] = residual
         total = total + jnp.sum(residual * residual, axis=1, keepdims=True)
     scale = lax.rsqrt(total * (1.0 / width) + 1e-06)
-    tokens[v] = (res_buf[...] * scale * gain_buf[...]).astype(jnp.bfloat16)
-    for i in range(1, n_view):
-        push(tokens.at[v], tokens.at[v], t_send.at[i], t_recv.at[i], view=view_at(i))
-    if gather:
-        for o in range(width // (per * HEAD_DIM) + 1, n_slab):
-            relay_z(UP, o)
-        for o in range(1, n_slab):
-            relay_z(DOWN, o)
-        for o in range(n_slab):
-            take_y(UP, o)
+    tokens[v] = (res_buf[...] * scale * gain_buf[...][None, :]).astype(jnp.bfloat16)
+    for i in [1] + list(range(2, n_view, 2)):
+        push(None, lambda: tokens.at[v], lambda: tokens.at[v], t_send.at[i], t_recv.at[i],
+             view=view_at(i))
+    if gather:
+        for hop in range(width // (per * HEAD_DIM) + 2, n_slab):
+            relay_z(UP, hop)
+        for hop in range(1, n_slab):
+            relay_z(DOWN, hop)
+        for hop in range(n_slab):
+            take_y(UP, hop)
     weight_loads[UP].wait()
 
     def unit(u):
@@ -348,26 +374,45 @@
         return lax.dot_general(hidden, down_buf[...], (((1,), (1,)), ((), ())),
                                preferred_element_type=jnp.float32).astype(jnp.bfloat16)
 
-    own_hidden = unit(v)
-    for i in range(1, n_view):
-        u = source_view(i)
-        landed(tokens.at[u], t_send.at[i], t_recv.at[i], view=u)
-        hidden = unit(u)
-        if i == 1:
-            weight_loads[DOWN].wait()
-            if gather:
-                for o in range(n_slab):
-                    take_y(DOWN, o)
-        terms[i] = term(hidden)
-        push(terms.at[i], sums.at[i], s_send.at[i], s_recv.at[i], view=u)
-    mixed = term(own_hidden).astype(jnp.float32)
-    for i in range(1, n_view):
-        landed(sums.at[i], s_send.at[i], s_recv.at[i], view=view_at(i))
+    def take_tokens(i):
+        landed(None, lambda: tokens.at[source_view(i)], t_send.at[i], t_recv.at[i],
+               view=source_view(i))
+
+    hidden = {0: unit(v)}
+    take_tokens(1)
+    hidden[1] = unit(partner)
+    for i in range(2, n_view, 2):
+        take_tokens(i)
+        part = lambda i=i: tokens.at[source_view(i)]
+        push(None, part, part, t_send.at[i + 1], t_recv.at[i + 1], view=partner)
+    for i in range(2, n_view, 2):
+        hidden[i] = unit(source_view(i))
+        take_tokens(i + 1)
+        hidden[i + 1] = unit(source_view(i + 1))
+    weight_loads[DOWN].wait()
+    if gather:
+        for hop in range(n_slab):
+            take_y(DOWN, hop)
+    for i in range(2, n_view, 2):
+        terms[i + 1] = term(hidden[i + 1])
+        push(None, lambda i=i: terms.at[i + 1], lambda i=i: sums.at[i + 1], s_send.at[i + 1],
+             s_recv.at[i + 1], view=partner)
+    for i in range(2, n_view, 2):
+        mine = term(hidden[i]).astype(jnp.float32)
+        landed(None, lambda: sums.at[i + 1], s_send.at[i + 1], s_recv.at[i + 1], view=partner)
+        terms[i] = (mine + sums[i + 1].astype(jnp.float32)).astype(jnp.bfloat16)
+        push(None, lambda i=i: terms.at[i], lambda i=i: sums.at[i], s_send.at[i], s_recv.at[i],
+             view=source_view(i))
+    terms[1] = term(hidden[1])
+    push(None, lambda: terms.at[1], lambda: sums.at[1], s_send.at[1], s_recv.at[1], view=partner)
+    mixed = term(hidden[0]).astype(jnp.float32)
+    for i in [1] + list(range(2, n_view, 2)):
+        landed(None, lambda: sums.at[i], s_send.at[i], s_recv.at[i], view=view_at(i))
         mixed = mixed + sums[i].astype(jnp.float32)
     out[...] = (res_buf[...] + mixed).astype(jnp.bfloat16)
 
-    for copy in sends:
-        copy.wait_send()
+    for cond, copy in sends:
+        only(cond, lambda: copy().wait_send())
     for i in range(1, n_view):
         feat_copy(i, 0).wait_send()
 
@@ -425,15 +470,15 @@
                 pltpu.VMEM((tokens, keys), jnp.float32),
                 pltpu.VMEM((tokens, width), half),
                 pltpu.VMEM((tokens, width), half),
-                pltpu.VMEM((1, width), jnp.float32),
+                pltpu.VMEM((width,), jnp.float32),
                 pltpu.VMEM((tokens, width), jnp.float32),
                 pltpu.VMEM((n_view, tokens, width), half),
                 pltpu.VMEM((n_view, tokens, width), half),
                 pltpu.VMEM((n_view, tokens, width), half),
                 dma((8,)),
-                dma((4, n_slab)), dma((4, n_slab)),
-                dma((4, n_dp, n_slab)), dma((4, n_dp, n_slab)),
-                dma((2, n_dp, n_slab)), dma((2, n_dp, n_slab)),
+                dma((4, 2, n_slab)), dma((4, 2, n_slab)),
+                dma((4, n_dp, 2, n_slab)), dma((4, n_dp, 2, n_slab)),
+                dma((2, n_dp, 2, n_slab)), dma((2, n_dp, 2, n_slab)),
                 dma((n_view, 3)), dma((n_view, 3)),
                 dma((n_view,)), dma((n_view,)),
                 dma((n_view,)), dma((n_view,)),
@@ -442,7 +487,7 @@
         )(
             latent_feats.reshape(tokens, channels), weights[0], weights[1],
             stream.reshape(tokens, width), queries.reshape(tokens, width),
-            norm_gain.reshape(1, width), weights[2], weights[3],
+            norm_gain, weights[2], weights[3],
             band_start, band_end, visibility,
         )
         return result.reshape(1, 1, row_count, col_count, width)

time: 71.4 us -> 61.1 us (0.86)
  Pallas kernels: 67.9 us -> 59.3 us
  local copies, waits for them, and re-layouts: 2.88 us -> 1.62 us
    pallas_call x1, Pallas kernels: 67.9 us -> 59.3 us  [shards(): pl.pallas_call(kernel, out_shape=jax.ShapeDtypeStruct((tokens, width), ha...]
    unnamed x3 -> x1, local copies, waits for them, and re-layouts: 2.3 us -> 1.62 us
where the time goes in v2:
time: 61.1 us; the launch traced here: 61 us
  Pallas kernels  59.3 us (97%)
  local copies, waits for them, and re-layouts  1.62 us (3%)
    pallas_call x1, Pallas kernels, shards(): pl.pallas_call(kernel, out_shape=jax.ShapeDtypeStruct((tokens, width), ha...  59.3 us
    unnamed x1, local copies, waits for them, and re-layouts  1.62 us

profile of v2, /device:TPU:0, one launch (start us, length us, event | category | flops | bytes accessed | tf_op | source)
XLA Modules:
  0.0 61.0 jit_solution(17374735301575752173)
XLA Ops:
  0.0 59.3 %shard_map.109 = bf16[128,768]{1,0:T(8,128)(2,1)} custom-call(bf16[128,256]{1,0:T(8,128)(2,1)} %bitcast.7, bf16[288,256]{1,0:T(8,128)(2,1)} %refs_1_.1, bf16[32,1536]{1,0:T(8,128)(2,1)} %refs_2_.1, bf16[128,768]{1,0:T(8,128)(2,1)} %bitcast.5, bf16[128,768]{1,0:T(8,128)(2,1)} %bitcast.6, f32[768]{0:T(1024)} %refs_5_.1, bf16[96,768]{1,0:T(8,128)(2,1)} %refs_6_.1, ...), custom_call_target="tpu_custom_call" | custom-call | tf_op jit(solution)/shard_map/pallas_call | solution.py:457
  59.4 1.6 %copy.13 = bf16[1,1,4,32,768]{4,3,2,1,0:T(8,128)(2,1)} copy(bf16[1,1,4,32,768]{4,3,2,1,0:T(8,128)(2,1)} %bitcast.4) | data formatting | bytes 393216
